TPU v7x, 512 devices: a whole 4x8x8 slice. The times are simulated.
512 devices in a mesh: band: 8 (over y_lo, core), row: 64 (over z, x, y_hi).
Axes of the slice: x: 4, y: 8 (y_hi: 2, y_lo: 4; y = y_hi * 4 + y_lo), z: 8, core: 2. Of those that a mesh axis runs over, the one named last changes fastest.
Arguments:
- pixels: float32 [512, 64, 7168], P('row', None, 'band'), may hold values from -6 to 6
- embed_weight: float32 [64, 64], replicated, may hold values from -0.75 to 0.75
- band_position_embedding: float32 [112, 64], replicated, may hold values from -6 to 6
- spec_qkv: float32 [64, 192], replicated, may hold values from -0.75 to 0.75
- spec_out: float32 [64, 64], replicated, may hold values from -0.75 to 0.75
- spec_scale: float32 [4], replicated, may hold values from 0.5 to 300, as said below
- spectral_up_weight: float32 [64, 256], replicated, may hold values from -0.75 to 0.75
- spectral_down_weight: float32 [256, 64], replicated, may hold values from -0.375 to 0.375
- pool_weight: float32 [12, 112], replicated, may hold values from -0.5 to 0.5
- qkv_weight: float32 [768, 2304], P(None, 'band'), may hold values from -0.21875 to 0.21875
- out_weight: float32 [768, 768], P(None, 'band'), may hold values from -0.21875 to 0.21875
- spat_scale: float32 [12], replicated, may hold values from 0.5 to 300, as said below
- shifts: int32 [2], replicated, may hold values from 1 to 7, as said below
Outputs:
- patch_out: float32 [512, 64, 768], P('row', 'band')
Inputs may be any that keep to these rules, and one draw needn't show every extreme that they name: shifts[0] rolls patch rows and lies in 1 to 7; shifts[1] rolls patch columns and lies in 1 to 7; the shift along the longer of the two (rows where 8 >= 8) is at its upper end. `spec_scale`: one positive scale per head. `spat_scale`: one positive scale per head.
All inputs are finite; a program needn't handle non-finite values.
Results may differ from a plain program's by a relative error of at most 0.0003.
Values sent between devices are 32-bit elements; how exact they have to be, the bound alone decides.
A program may use at most 64 MiB of HBM per device.

v0:
```python
import math

import jax
import jax.numpy as jnp
from jax import lax
from jax.sharding import PartitionSpec as P

WIN = 8


highest_precision = lax.Precision.HIGHEST
epsilon = 1e-05


def from_behind(block, axis, distance):
    devices = range(lax.axis_size(axis))
    route = [((i - distance) % len(devices), i) for i in devices]
    return lax.ppermute(block, axis, route)


def layer_normalize(values):
    average = jnp.mean(values, axis=-1, keepdims=True)
    centred = values - average
    spread = jnp.mean(centred * centred, axis=-1, keepdims=True)
    return centred * lax.rsqrt(spread + epsilon)


def stable_softmax(scores):
    top_score = jnp.max(scores, axis=-1, keepdims=True)
    shifted = jnp.exp(scores - top_score)
    return shifted / jnp.sum(shifted, axis=-1, keepdims=True)


def spectral_row(
    patch_row,
    embed_weight,
    band_position_embedding,
    spec_qkv,
    spec_out,
    spec_scale,
    spectral_up_weight,
    spectral_down_weight,
    pool_weight,
):
    patch_count = patch_row.shape[0]
    band_count = band_position_embedding.shape[0]
    token_width = band_position_embedding.shape[1]
    pixel_count = embed_weight.shape[0]
    head_count = spec_scale.shape[0]
    head_size = token_width // head_count
    raw_tokens = patch_row.reshape(patch_count, band_count, pixel_count)
    tokens = (
        jnp.einsum("cbp,pw->cbw", raw_tokens, embed_weight, precision=highest_precision)
        + band_position_embedding
    )
    projected = jnp.einsum(
        "cbw,wk->cbk", layer_normalize(tokens), spec_qkv, precision=highest_precision
    )
    shaped = projected.reshape(patch_count, band_count, 3, head_count, head_size)
    scores = jnp.einsum(
        "cqhd,ckhd->chqk", shaped[:, :, 0], shaped[:, :, 1], precision=highest_precision
    )
    scores = scores * (spec_scale / math.sqrt(head_size))[:, None, None]
    attention = stable_softmax(scores)
    mixed = jnp.einsum("chqk,ckhd->cqhd", attention, shaped[:, :, 2], precision=highest_precision)
    mixed = mixed.reshape(patch_count, band_count, token_width)
    running_state = tokens + jnp.einsum("cbw,wv->cbv", mixed, spec_out, precision=highest_precision)
    hidden_activations = jax.nn.gelu(
        jnp.einsum(
            "sio,or->sir",
            layer_normalize(running_state),
            spectral_up_weight,
            precision=highest_precision,
        )
    )
    running_state = running_state + jnp.einsum(
        "rgp,pu->rgu", hidden_activations, spectral_down_weight, precision=highest_precision
    )
    pooled = jnp.einsum("gb,cbw->cgw", pool_weight, running_state, precision=highest_precision)
    return pooled.reshape(patch_count, pool_weight.shape[0] * token_width)


def to_windows(grid, window):
    grid_rows, grid_cols, feature_width = grid.shape
    shaped = grid.reshape(grid_rows // window, window, grid_cols // window, window, feature_width)
    return shaped.transpose(0, 2, 1, 3, 4).reshape(-1, window * window, feature_width)


def from_windows(windows, grid_rows, grid_cols, window):
    feature_width = windows.shape[-1]
    shaped = windows.reshape(
        grid_rows // window, grid_cols // window, window, window, feature_width
    )
    return shaped.transpose(0, 2, 1, 3, 4).reshape(grid_rows, grid_cols, feature_width)


def window_attention(projected, labels, spat_scale, window_count, window_area):
    model_width = projected.shape[1] // 3
    head_count = spat_scale.shape[0]
    head_size = model_width // head_count
    shaped = projected.reshape(window_count, window_area, 3, head_count, head_size)
    scores = jnp.einsum(
        "wqhd,wkhd->whqk", shaped[:, :, 0], shaped[:, :, 1], precision=highest_precision
    )
    scores = scores * (spat_scale / math.sqrt(head_size))[:, None, None]
    same_region = labels[:, :, None] == labels[:, None, :]
    scores = jnp.where(same_region[:, None], scores, -1e30)
    attention = stable_softmax(scores)
    mixed = jnp.einsum("whqk,wkhd->wqhd", attention, shaped[:, :, 2], precision=highest_precision)
    return mixed.reshape(window_count * window_area, model_width)


def project(tokens, weight_part):
    return jnp.dot(
        tokens, weight_part, precision=highest_precision, preferred_element_type=jnp.float32
    )


def on_device(
    pixels,
    embed_weight,
    band_position_embedding,
    spec_qkv,
    spec_out,
    spec_scale,
    spectral_up_weight,
    spectral_down_weight,
    pool_weight,
    qkv_weight,
    out_weight,
    spat_scale,
    shifts,
):
    weight_sets = (
        lax.all_gather(qkv_weight, "band", axis=1, tiled=True),
        lax.all_gather(out_weight, "band", axis=1, tiled=True),
    )

    def one_row(patch_row):
        return spectral_row(
            patch_row,
            embed_weight,
            band_position_embedding,
            spec_qkv,
            spec_out,
            spec_scale,
            spectral_up_weight,
            spectral_down_weight,
            pool_weight,
        )

    pooled = lax.map(
        one_row, lax.all_to_all(pixels, "band", split_axis=1, concat_axis=2, tiled=True)
    )
    strip_rows = pooled.shape[0]
    strip_cols = pooled.shape[1]
    model_width = pooled.shape[2]
    shift_rows = shifts[0]
    shift_cols = shifts[1]
    lower_strip_rows = from_behind(pooled, "row", -1)
    stacked = jnp.concatenate([pooled, lower_strip_rows], 0)
    right_block = from_behind(stacked, "band", -1)
    square = jnp.concatenate([stacked, right_block], 1)
    rolled = lax.dynamic_slice(
        square,
        (shift_rows, shift_cols, jnp.zeros((), jnp.int32)),
        (strip_rows, strip_cols, model_width),
    )
    row_index = lax.axis_index("row") * strip_rows + jnp.arange(strip_rows, dtype=jnp.int32)
    col_index = lax.axis_index("band") * strip_cols + jnp.arange(strip_cols, dtype=jnp.int32)
    row_region = (row_index >= lax.axis_size("row") * strip_rows - shift_rows).astype(jnp.int32)
    col_region = (col_index >= lax.axis_size("band") * strip_cols - shift_cols).astype(jnp.int32)
    labels = (2 * row_region[:, None] + col_region[None, :])[:, :, None]
    windows = to_windows(rolled, WIN)
    label_windows = to_windows(labels, WIN)[:, :, 0]
    flat_tokens = windows.reshape(-1, model_width)
    projected = project(layer_normalize(flat_tokens), weight_sets[0])
    mixed = window_attention(projected, label_windows, spat_scale, windows.shape[0], WIN * WIN)
    result = flat_tokens + project(mixed, weight_sets[1])
    return from_windows(result.reshape(windows.shape), strip_rows, strip_cols, WIN)


def solution(mesh):
    return jax.shard_map(
        on_device,
        mesh=mesh,
        in_specs=(
            P("row", None, "band"),
            P(),
            P(),
            P(),
            P(),
            P(),
            P(),
            P(),
            P(),
            P(None, "band"),
            P(None, "band"),
            P(),
            P(),
        ),
        out_specs=P("row", "band", None),
        check_vma=False,
    )
```

profile of v0, /device:TPU:1, one launch (start us, length us, event | category | flops | bytes accessed | tf_op | source)
XLA Modules:
  0.0 244.5 jit_solution(16165410811291617363)
XLA Ops:
  7.3 3.8 %copy.36 = f32[8,64,896]{2,0,1:T(8,128)} copy(f32[8,64,896]{2,1,0:T(8,128)} %param.15) | data formatting | bytes 3670016 | tf_op args[0]
  11.0 10.5 %all-to-all-start = ((f32[8,64,896]{2,0,1:T(8,128)}), f32[8,64,896]{2,0,1:T(8,128)S(1)}, u32[]{:S(2)}, u32[]{:S(2)}) async-start(f32[8,64,896]{2,0,1:T(8,128)} %copy.36), calls=%async_computation | async-start | bytes 3670016 | tf_op jit(solution)/shard_map/all_to_all | solution.py:153
  24.3 63.0 %all-to-all-done = f32[8,64,896]{2,0,1:T(8,128)S(1)} async-done(((f32[8,64,896]{2,0,1:T(8,128)}), f32[8,64,896]{2,0,1:T(8,128)S(1)}, u32[]{:S(2)}, u32[]{:S(2)}) %all-to-all-start) | async-done | bytes 1835040 | tf_op jit(solution)/shard_map/all_to_all | solution.py:153
  87.3 1.6 copy.37
  88.9 96.4 %while.10 = (s32[]{:T(128)}, f32[8,8,768]{2,1,0:T(8,128)S(1)}, f32[8,8,7168]{2,1,0:T(8,128)}, f32[64,64]{0,1:T(8,128)S(1)}, f32[112,64]{0,1:T(8,128)S(1)}, /*ind...) while((s32[]{:T(128)}, f32[8,8,768]{2,1,0:T(8,128)S(1)}, ...), condition=%wide.region_7.8_spmd, body=%wide.region_0.7_spmd.sunk | while | flops 740821760 | bytes 12766637 | solution.py:152
  90.0 1.0 fusion.83
  92.0 3.1 %multiply_reduce_fusion.8 = (f32[8,4,112]{2,1,0:T(4,128)S(1)}, f32[8,4,112,112]{2,3,1,0:T(8,128)S(1)}) fusion(f32[4]{0:T(128)S(1)} %broadcast_multiply_fusion.8, f32[8,112,3,4,16]{1,4,3,2,0:T(8,128)S(1)} %bitcast.135), kind=kOutput, calls=%fused_computation.3.clone.1 | convolution fusion | flops 77869568 | bytes 2144768 | tf_op jit(solution)/shard_map/while/body/eval_jaxpr/cqhd,ckhd->chqk/dot_general | solution.py:60
  95.6 1.9 fusion.86
  98.0 1.1 fusion.88
  99.1 1.1 convolution_add_fusion.4
  104.0 3.1 %multiply_reduce_fusion.8 = (f32[8,4,112]{2,1,0:T(4,128)S(1)}, f32[8,4,112,112]{2,3,1,0:T(8,128)S(1)}) fusion(f32[4]{0:T(128)S(1)} %broadcast_multiply_fusion.8, f32[8,112,3,4,16]{1,4,3,2,0:T(8,128)S(1)} %bitcast.135), kind=kOutput, calls=%fused_computation.3.clone.1 | convolution fusion | flops 77869568 | bytes 2144768 | tf_op jit(solution)/shard_map/while/body/eval_jaxpr/cqhd,ckhd->chqk/dot_general | solution.py:60
  107.6 1.9 fusion.86
  110.0 1.1 fusion.88
  111.1 1.1 convolution_add_fusion.4
  114.1 1.0 fusion.83
  116.1 3.1 %multiply_reduce_fusion.8 = (f32[8,4,112]{2,1,0:T(4,128)S(1)}, f32[8,4,112,112]{2,3,1,0:T(8,128)S(1)}) fusion(f32[4]{0:T(128)S(1)} %broadcast_multiply_fusion.8, f32[8,112,3,4,16]{1,4,3,2,0:T(8,128)S(1)} %bitcast.135), kind=kOutput, calls=%fused_computation.3.clone.1 | convolution fusion | flops 77869568 | bytes 2144768 | tf_op jit(solution)/shard_map/while/body/eval_jaxpr/cqhd,ckhd->chqk/dot_general | solution.py:60
  119.7 1.9 fusion.86
  122.1 1.1 fusion.88
  123.2 1.1 convolution_add_fusion.4
  126.2 1.0 fusion.83
  128.1 3.1 %multiply_reduce_fusion.8 = (f32[8,4,112]{2,1,0:T(4,128)S(1)}, f32[8,4,112,112]{2,3,1,0:T(8,128)S(1)}) fusion(f32[4]{0:T(128)S(1)} %broadcast_multiply_fusion.8, f32[8,112,3,4,16]{1,4,3,2,0:T(8,128)S(1)} %bitcast.135), kind=kOutput, calls=%fused_computation.3.clone.1 | convolution fusion | flops 77869568 | bytes 2144768 | tf_op jit(solution)/shard_map/while/body/eval_jaxpr/cqhd,ckhd->chqk/dot_general | solution.py:60
  131.7 1.9 fusion.86
  134.1 1.1 fusion.88
  135.2 1.1 convolution_add_fusion.4
  138.2 1.0 fusion.83
  140.2 3.1 %multiply_reduce_fusion.8 = (f32[8,4,112]{2,1,0:T(4,128)S(1)}, f32[8,4,112,112]{2,3,1,0:T(8,128)S(1)}) fusion(f32[4]{0:T(128)S(1)} %broadcast_multiply_fusion.8, f32[8,112,3,4,16]{1,4,3,2,0:T(8,128)S(1)} %bitcast.135), kind=kOutput, calls=%fused_computation.3.clone.1 | convolution fusion | flops 77869568 | bytes 2144768 | tf_op jit(solution)/shard_map/while/body/eval_jaxpr/cqhd,ckhd->chqk/dot_general | solution.py:60
  143.8 1.9 fusion.86
  146.2 1.1 fusion.88
  147.3 1.1 convolution_add_fusion.4
  150.3 1.0 fusion.83
  152.2 3.1 %multiply_reduce_fusion.8 = (f32[8,4,112]{2,1,0:T(4,128)S(1)}, f32[8,4,112,112]{2,3,1,0:T(8,128)S(1)}) fusion(f32[4]{0:T(128)S(1)} %broadcast_multiply_fusion.8, f32[8,112,3,4,16]{1,4,3,2,0:T(8,128)S(1)} %bitcast.135), kind=kOutput, calls=%fused_computation.3.clone.1 | convolution fusion | flops 77869568 | bytes 2144768 | tf_op jit(solution)/shard_map/while/body/eval_jaxpr/cqhd,ckhd->chqk/dot_general | solution.py:60
  155.8 1.9 fusion.86
  158.2 1.1 fusion.88
  159.3 1.1 convolution_add_fusion.4
  162.3 1.0 fusion.83
  164.3 3.1 %multiply_reduce_fusion.8 = (f32[8,4,112]{2,1,0:T(4,128)S(1)}, f32[8,4,112,112]{2,3,1,0:T(8,128)S(1)}) fusion(f32[4]{0:T(128)S(1)} %broadcast_multiply_fusion.8, f32[8,112,3,4,16]{1,4,3,2,0:T(8,128)S(1)} %bitcast.135), kind=kOutput, calls=%fused_computation.3.clone.1 | convolution fusion | flops 77869568 | bytes 2144768 | tf_op jit(solution)/shard_map/while/body/eval_jaxpr/cqhd,ckhd->chqk/dot_general | solution.py:60
  167.9 1.9 fusion.86
  170.3 1.1 fusion.88
  171.4 1.1 convolution_add_fusion.4
  176.4 3.1 %multiply_reduce_fusion.8 = (f32[8,4,112]{2,1,0:T(4,128)S(1)}, f32[8,4,112,112]{2,3,1,0:T(8,128)S(1)}) fusion(f32[4]{0:T(128)S(1)} %broadcast_multiply_fusion.8, f32[8,112,3,4,16]{1,4,3,2,0:T(8,128)S(1)} %bitcast.135), kind=kOutput, calls=%fused_computation.3.clone.1 | convolution fusion | flops 77869568 | bytes 2144768 | tf_op jit(solution)/shard_map/while/body/eval_jaxpr/cqhd,ckhd->chqk/dot_general | solution.py:60
  179.9 1.9 fusion.86
  182.3 1.1 fusion.88
  183.4 1.1 convolution_add_fusion.4
  185.3 14.8 %collective-permute-start = (f32[8,8,768]{2,1,0:T(8,128)S(1)}, f32[8,8,768]{2,1,0:T(8,128)S(1)}, u32[]{:S(2)}, u32[]{:S(2)}) collective-permute-start(f32[8,8,768]{2,1,0:T(8,128)S(1)} %get-tuple-element.62), channel_id=1, source_target_pairs={{1,0},{2,1},{3,2},{4,3},{5,4},{6,5},{7,6},{8,7},{9,8},{10,9},{11,1... | collective-permute-start | bytes 589832 | tf_op jit(solution)/shard_map/ppermute | solution.py:18
  204.1 4.9 %collective-permute-start.1 = (f32[16,8,768]{2,1,0:T(8,128)S(1)}, f32[16,8,768]{2,1,0:T(8,128)S(1)}, u32[]{:S(2)}, u32[]{:S(2)}) collective-permute-start(f32[16,8,768]{2,1,0:T(8,128)S(1)} %constant_dynamic-update-slice_fusion.1), channel_id=1, source_target_pairs={{64,0},{128,64},{192,128},{256,192},{320,256},{384,320},{448,384},... | collective-permute-start | bytes 1179656 | tf_op jit(solution)/shard_map/ppermute | solution.py:18
  209.1 9.3 %collective-permute-done.1 = f32[16,8,768]{2,1,0:T(8,128)S(1)} collective-permute-done((f32[16,8,768]{2,1,0:T(8,128)S(1)}, f32[16,8,768]{2,1,0:T(8,128)S(1)}, u32[]{:S(2)}, u32[]{:S(2)}) %collective-permute-start.1) | collective-permute-done | bytes 393248 | tf_op jit(solution)/shard_map/ppermute | solution.py:18
  218.9 12.6 %convolution_bitcast_fusion.1 = f32[1,64,3,12,64]{4,1,3,2,0:T(8,128)S(1)} fusion(f32[3,12,64,768]{3,2,1,0:T(8,128)} %bitcast.138, f32[8,8,768]{2,1,0:T(8,128)S(1)} %get-tuple-element.119, f32[64]{0:T(128)S(1)} %rsqrt.28, f32[64]{0:T(128)S(1)} %div.44), kind=kOutput, calls=%fused_computation.48 | convolution fusion | flops 1359052800 | bytes 7864832 | tf_op jit(solution)/shard_map/dot_general | solution.py:114
  233.2 4.5 %fusion.37 = f32[8,8,768]{2,1,0:T(8,128)} fusion(f32[8,8,768]{2,1,0:T(8,128)S(1)} %get-tuple-element.119, f32[64,768]{0,1:T(8,128)S(1)} %bitcast.141, f32[768,768]{0,1:T(8,128)} %all-gather.5.cloned.1.call-done), kind=kOutput, calls=%fused_computation.65 | convolution fusion | flops 453033984 | bytes 2949120 | tf_op jit(solution)/shard_map/dot_general | solution.py:114
  (170 shorter events, 36.5 us)
Async XLA Ops:
  6.5 212.3 %all-gather.3.cloned.1.call-start = ((), (), s32[]{:S(2)}) async-start(), calls=%async_computation.1 | async-start | bytes 7962624 | tf_op jit(solution)/shard_map/all_gather | solution.py:135
  11.0 11.2 %copy-start.4 = (f32[64,64]{1,0:T(8,128)S(1)}, f32[64,64]{1,0:T(8,128)}, u32[]{:S(2)}) copy-start(f32[64,64]{1,0:T(8,128)} %param.16) | copy-start | bytes 49156
  11.0 11.3 %copy-start.5 = (f32[64,64]{1,0:T(8,128)S(1)}, f32[64,64]{1,0:T(8,128)}, u32[]{:S(2)}) copy-start(f32[64,64]{1,0:T(8,128)} %param.19) | copy-start | bytes 49156
  11.0 11.4 %copy-start.6 = (s32[2]{0:T(128)S(1)}, s32[2]{0:T(128)}, u32[]{:S(2)}) copy-start(s32[2]{0:T(128)} %param.27) | copy-start | bytes 28
  11.0 76.2 %all-to-all-start = ((f32[8,64,896]{2,0,1:T(8,128)}), f32[8,64,896]{2,0,1:T(8,128)S(1)}, u32[]{:S(2)}, u32[]{:S(2)}) async-start(f32[8,64,896]{2,0,1:T(8,128)} %copy.36), calls=%async_computation | async-start | bytes 3670016 | tf_op jit(solution)/shard_map/all_to_all | solution.py:153
  21.5 211.6 %all-gather.5.cloned.1.call-start = ((), (), s32[]{:S(2)}) async-start(), calls=%async_computation.2 | async-start | bytes 2654208 | tf_op jit(solution)/shard_map/all_gather | solution.py:136
  87.3 1.6 copy-start
  87.3 1.6 copy-start.1
  87.3 1.6 copy-start.2
  87.3 1.6 copy-start.3
  87.3 1.6 copy-start.7
  87.3 1.6 copy-start.8
  88.9 120.1 %copy-start.9 = (f32[12]{0:T(128)S(1)}, f32[12]{0:T(128)}, u32[]{:S(2)}) copy-start(f32[12]{0:T(128)} %param.26) | copy-start | bytes 148
  185.3 18.7 %collective-permute-start = (f32[8,8,768]{2,1,0:T(8,128)S(1)}, f32[8,8,768]{2,1,0:T(8,128)S(1)}, u32[]{:S(2)}, u32[]{:S(2)}) collective-permute-start(f32[8,8,768]{2,1,0:T(8,128)S(1)} %get-tuple-element.62), channel_id=1, source_target_pairs={{1,0},{2,1},{3,2},{4,3},{5,4},{6,5},{7,6},{8,7},{9,8},{10,9},{11,1... | collective-permute-start | bytes 589832 | tf_op jit(solution)/shard_map/ppermute | solution.py:18
  204.1 14.3 %collective-permute-start.1 = (f32[16,8,768]{2,1,0:T(8,128)S(1)}, f32[16,8,768]{2,1,0:T(8,128)S(1)}, u32[]{:S(2)}, u32[]{:S(2)}) collective-permute-start(f32[16,8,768]{2,1,0:T(8,128)S(1)} %constant_dynamic-update-slice_fusion.1), channel_id=1, source_target_pairs={{64,0},{128,64},{192,128},{256,192},{320,256},{384,320},{448,384},... | collective-permute-start | bytes 1179656 | tf_op jit(solution)/shard_map/ppermute | solution.py:18
Sparse Core Ops, SparseCore 0:
  9.4 116.9 all-gather.2
  128.5 43.3 all-gather.4
where the time goes:
time: 245 us
  matrix products  100 us (41%)
  waiting for transfers between devices  73.7 us (30%)
  starting transfers between devices  30.1 us (12%)
  between operations  18.6 us (8%)
  local copies, waits for them, and re-layouts  15.8 us (6%)
  other arithmetic  5.39 us (2%)
    all_to_all x1, waiting for transfers between devices, on_device(): lax.all_to_all(pixels, 'band', split_axis=1, concat_axis=2, tiled=True)  63 us
    dot_general x8, matrix products, spectral_row(): jnp.einsum('cqhd,ckhd->chqk', shaped[:, :, 0], shaped[:, :, 1], precision...  24.8 us
    ppermute x2, starting transfers between devices, from_behind(): return lax.ppermute(block, axis, route)  19.7 us
    dot_general x2, matrix products, project(): jnp.dot(tokens, weight_part, precision=highest_precision, preferred_eleme...  17.1 us
    dot_general x8, matrix products, spectral_row(): jnp.einsum('chqk,ckhd->cqhd', attention, shaped[:, :, 2], precision=highe...  15.3 us
    all_to_all x1, starting transfers between devices, on_device(): lax.all_to_all(pixels, 'band', split_axis=1, concat_axis=2, tiled=True)  10.5 us
    ppermute x2, waiting for transfers between devices, from_behind(): return lax.ppermute(block, axis, route)  9.26 us
    dot_general x8, matrix products, spectral_row(): jnp.einsum('sio,or->sir', layer_normalize(running_state), spectral_up_wei...  8.84 us
  transfers between devices with their start and end apart: 5, of which 2 were waited for; matrix products, arithmetic and copies ran while one was open for 48% of the time, Pallas kernels for 0%

commit v1 on v0

v1 whole, which is shorter than its diff:
```python
import math
import jax, jax.numpy as jnp
from jax import lax
from jax.experimental import pallas as pl
from jax.experimental.pallas import tpu as pltpu

F32, BF16 = jnp.float32, jnp.bfloat16
EPS = 1e-05

def parts(x, n):
    out = []
    for i in range(n):
        p = x.astype(BF16)
        out.append(p)
        if i < n - 1:
            x = x - p.astype(F32)
    return out

def wparts(w, n):
    out = []
    for i in range(n):
        p = lax.reduce_precision(w, 8, 7)
        out.append(p.astype(BF16))
        w = w - p
    return out

def lhs6(x, axis=1):
    a, b, c = parts(x, 3)
    return jnp.concatenate([a, b, c, a, b, a], axis)

def rhs6(w, axis=0):
    a, b, c = wparts(w, 3)
    return jnp.concatenate([a, a, a, b, b, c], axis)

def lhs3(x, axis=1):
    a, b = parts(x, 2)
    return jnp.concatenate([a, b, a], axis)

def rhs3(w, axis=0):
    a, b = wparts(w, 2)
    return jnp.concatenate([a, a, b], axis)

def mm(a, b, ca=1, cb=0):
    return lax.dot_general(a, b, (((ca,), (cb,)), ((), ())), preferred_element_type=F32)

def bd(w):
    z = jnp.zeros_like(w)
    return jnp.concatenate([jnp.concatenate([w, z], 1), jnp.concatenate([z, w], 1)], 0)

def prepare(embed, bpos, qkv, out, sscale, up, down, pool):
    cent = lambda w: w - jnp.mean(w, axis=1, keepdims=True)
    cat = jnp.concatenate
    we = cat([bd(embed), bd(cent(embed))], 1)
    bp = cat([bpos.reshape(56, 128), cent(bpos).reshape(56, 128)], 1)
    qs = jnp.repeat(sscale * (math.log2(math.e) / 4.0), 16)[None, :]
    q, k, v = qkv[:, :64] * qs, qkv[:, 64:128], qkv[:, 128:]
    w1, w2, w3 = wparts(cat([q, k, v, v], 1), 3)
    wq = cat([w1, w1, w2, w2, w1, w3], 0)
    wo = rhs3(cat([bd(out), bd(cent(out))], 1))
    u1, u2 = wparts(up, 2)
    wu = cat([u1, u1, u2, u2], 0)
    d1, d2 = wparts(bd(down), 2)
    wd = cat([cat([d1, d2], 1), cat([d1, jnp.zeros_like(d1)], 1)], 0)
    g = pool.reshape(12, 56, 2).transpose(0, 2, 1)
    e8 = jnp.eye(8, dtype=F32)
    gp = (g[:, :, None, None, :] * e8[None, None, :, :, None]).reshape(192, 448)
    gp = jnp.stack(wparts(gp, 2))
    return (rhs6(we), bp, wq, wo, wu, wd, gp)

def gelu(v):
    return 0.5 * v * (1.0 + jnp.tanh(math.sqrt(2 / math.pi) * (v + 0.044715 * (v * v * v))))

def row_tokens(load, we_ref, bp_ref, wq_ref, wo_ref, wu_ref, wd_ref, gp_ref):
    NP = 8
    cat = jnp.concatenate
    x = cat([load(p) for p in range(NP)], 0)
    bpt = cat([bp_ref[...]] * NP, 0)
    t = mm(lhs6(x), we_ref[...]) + bpt
    tok, tokc = t[:, :128], t[:, 128:]
    r_i = lax.broadcasted_iota(jnp.int32, (128, 128), 0) // 64
    c_i = lax.broadcasted_iota(jnp.int32, (128, 128), 1) // 64
    avg = jnp.where(r_i == c_i, 1.0 / 64, 0.0).astype(BF16)
    avg = cat([avg, avg], 0)
    low = lax.broadcasted_iota(jnp.int32, (448, 128), 1) < 64

    def norm(c):
        var = mm(cat(parts(c * c, 2), 1), avg)
        return c * lax.rsqrt(var + EPS)

    def split_bands(n, k):
        ps = [a.astype(F32) for a in parts(n, k)]
        rs = [pltpu.roll(a, 64, 1) for a in ps]
        pairs = [(0, 1)] + ([(2, 0)] if k == 3 else [])
        b0 = [jnp.where(low, ps[i], rs[j]).astype(BF16) for i, j in pairs]
        b1 = [jnp.where(low, rs[i], ps[j]).astype(BF16) for i, j in pairs]
        return cat([cat([b[0]] + b, 1) for b in (b0, b1)], 0)

    qkv = mm(split_bands(norm(tokc), 3), wq_ref[...])
    lane = lax.broadcasted_iota(jnp.int32, (1, 128), 1)
    lowp = lax.broadcasted_iota(jnp.int32, (112, 128), 1) < 64
    mlow = jnp.where(lane < 64, 1.0, 0.0).astype(BF16)
    mhigh = jnp.where(lane < 64, 0.0, 1.0).astype(BF16)
    hm = [jnp.where((lane // 16) % 4 == h, 1.0, 0.0).astype(BF16) for h in range(4)]
    row128 = lax.broadcasted_iota(jnp.int32, (128, 112), 0)
    mixes = []
    for p in range(NP):
        def both(sl):
            return cat([qkv[56 * p:56 * p + 56, sl], qkv[448 + 56 * p:504 + 56 * p, sl]], 0)
        qk, v = both(slice(0, 128)), both(slice(128, 256))
        kq = pltpu.roll(qk, 64, 1)
        q1, q2, q3 = parts(jnp.where(lowp, qk, kq), 3)
        k1, k2, k3 = parts(jnp.where(lowp, kq, qk), 3)
        kl = k1 * mlow + k2 * mhigh
        lhs = cat([kl, kl, k1 * mlow + k3 * mhigh], 1)
        qc = cat([q1, q2, q3 * mlow + q1 * mhigh], 1)
        pad = jnp.zeros((16, 384), BF16)
        heads = []
        for h in range(4):
            heads += [qc * cat([hm[h]] * 3, 1), pad]
        st = mm(lhs, cat(heads, 0), 1, 1)
        m = jnp.max(st, axis=0, keepdims=True)
        e = jnp.exp2(st - m)
        s = jnp.sum(e, axis=0, keepdims=True)
        e1, e2 = parts(e, 2)
        vt = v.T
        vh = vt.astype(BF16).astype(F32)
        vs = jnp.where(row128 < 64, vh, vt - vh).astype(BF16)
        r = mm(vs, e1)
        r2 = mm(vs[:64], e2)
        inv = 1.0 / s
        ot = []
        for h in range(4):
            sl = slice(128 * h, 128 * h + 128)
            o = r[16 * h:16 * h + 16, sl] + r[64 + 16 * h:80 + 16 * h, sl] + r2[16 * h:16 * h + 16, sl]
            ot.append(o * inv[:, sl])
        mt = cat(ot, 0)
        mt = cat([mt, pltpu.roll(mt, 72, 1)], 0)
        mixes.append(mt.T[:56])
    mix = cat(mixes, 0)
    o = mm(lhs3(mix), wo_ref[...])
    n2 = norm(tokc + o[:, 128:])
    h = gelu(mm(split_bands(n2, 2), wu_ref[...]))
    h1, h2 = parts(h, 2)
    hc = cat([h1[:448], h1[448:], h2[:448], h2[448:]], 1)
    d = mm(hc, wd_ref[...])
    y = tok + o[:, :128] + (d[:, :128] + d[:, 128:])
    y1, y2 = parts(y, 2)
    r = mm(gp_ref[0], cat([y1, y2], 1))
    r = (r[:, :128] + r[:, 128:]) + mm(gp_ref[1], y1)
    lo8 = lax.broadcasted_iota(jnp.int32, (8, 128), 1) < 64
    outs = []
    for j in range(6):
        g = lambda a, b: r[((2 * j + a) * 2 + b) * 8:((2 * j + a) * 2 + b) * 8 + 8]
        outs.append(jnp.where(lo8, g(0, 0) + pltpu.roll(g(0, 1), 64, 1),
                              pltpu.roll(g(1, 0), 64, 1) + g(1, 1)))
    return cat(outs, 1)


def spread_kernel(px, we, bp, wq, wo, wu, wd, gp, out, xbuf, zs, lsem, ssem, rsem, zsem, zrem, fsem, frem):
    nb, nr = lax.axis_size("band"), lax.axis_size("row")
    me, row = lax.axis_index("band"), lax.axis_index("row")
    up = lax.rem(row + nr - 1, nr)
    down = lax.rem(row + 1, nr)
    left = lax.rem(me + nb - 1, nb)
    MESH = pl.DeviceIdType.MESH
    barrier = pltpu.get_barrier_semaphore()
    for k in range(1, nb):
        pl.semaphore_signal(barrier, inc=1, device_id={"band": lax.rem(me + k, nb)}, device_id_type=MESH)
    pl.semaphore_signal(barrier, inc=1, device_id={"row": down}, device_id_type=MESH)

    def own(r):
        return pltpu.make_async_copy(px.at[r, me], xbuf.at[r, pl.ds(me * 56, 56)], lsem.at[r])

    def hop(r, k):
        to = lax.rem(me + k, nb)
        return pltpu.make_async_remote_copy(
            src_ref=px.at[r, to], dst_ref=xbuf.at[r, pl.ds(me * 56, 56)],
            send_sem=ssem.at[r, k], recv_sem=rsem.at[r, k],
            device_id={"band": to}, device_id_type=MESH)

    def rise(r):
        return pltpu.make_async_remote_copy(
            src_ref=zs.at[r], dst_ref=out.at[r + 1, pl.ds(0, 8)],
            send_sem=zsem.at[r], recv_sem=zrem.at[r], device_id={"row": up}, device_id_type=MESH)

    def side(r):
        return pltpu.make_async_remote_copy(
            src_ref=out.at[r, pl.ds(0, 8)], dst_ref=out.at[r, pl.ds(8, 8)],
            send_sem=fsem.at[r], recv_sem=frem.at[r], device_id={"band": left}, device_id_type=MESH)

    def start_own(r, c):
        own(r).start()
        return c
    lax.fori_loop(0, 8, start_own, 0)
    pl.semaphore_wait(barrier, nb)

    def start_row(r, c):
        for k in ORDER:
            hop(r, k).start()
        return c
    lax.fori_loop(0, 8, start_row, 0)

    def one(r, c):
        own(r).wait()
        for k in range(1, nb):
            hop(r, k).wait_recv()
        z = row_tokens(lambda p: xbuf[r, pl.ds(p, 56, stride=8), :], we, bp, wq, wo, wu, wd, gp)

        @pl.when(r < 7)
        def _():
            zs[r] = z
            rise(r).start()

        @pl.when(r == 7)
        def _():
            out[0, 0:8] = z
            side(0).start()

        @pl.when(r > 0)
        def _():
            rise(r - 1).wait_recv()
            side(r).start()
        return c
    lax.fori_loop(0, 8, one, 0)

    def finish(r, c):
        for k in range(1, nb):
            hop(r, k).wait_send()
        side(r).wait()

        @pl.when(r < 7)
        def _():
            rise(r).wait_send()
        return c
    lax.fori_loop(0, 8, finish, 0)


ORDER = (4, 3, 5, 2, 6, 1, 7)


def spread(px, *ws):
    V = pl.BlockSpec(memory_space=pltpu.VMEM)
    D = pltpu.SemaphoreType.DMA
    return pl.pallas_call(
        spread_kernel,
        out_shape=jax.ShapeDtypeStruct((8, 16, 768), F32),
        in_specs=[pl.BlockSpec(memory_space=pl.ANY)] + [V] * 7,
        out_specs=V,
        scratch_shapes=[pltpu.VMEM((8, 448, 128), F32), pltpu.VMEM((8, 8, 768), F32),
                        D((8,)), D((8, 8)), D((8, 8)), D((8,)), D((8,)), D((8,)), D((8,))],
        compiler_params=pltpu.CompilerParams(collective_id=0, has_side_effects=True,
                                             vmem_limit_bytes=40 * 2 ** 20),
        name="spread",
    )(px, *ws)


highest_precision = lax.Precision.HIGHEST


def layer_normalize(values):
    average = jnp.mean(values, axis=-1, keepdims=True)
    centred = values - average
    spread_ = jnp.mean(centred * centred, axis=-1, keepdims=True)
    return centred * lax.rsqrt(spread_ + EPS)


def window_attention(projected, same, spat_scale):
    shaped = projected.reshape(64, 3, 12, 64)
    scores = jnp.einsum("qhd,khd->hqk", shaped[:, 0], shaped[:, 1], precision=highest_precision)
    scores = scores * (spat_scale / math.sqrt(64))[:, None, None]
    scores = jnp.where(same[None], scores, -1e30)
    top = jnp.max(scores, axis=-1, keepdims=True)
    e = jnp.exp(scores - top)
    a = e / jnp.sum(e, axis=-1, keepdims=True)
    return jnp.einsum("hqk,khd->qhd", a, shaped[:, 2], precision=highest_precision).reshape(64, 768)


def on_device(pixels, embed, bpos, qkv, out, sscale, upw, downw, pool, qkv_weight, out_weight, spat_scale, shifts):
    w_qkv = lax.all_gather(qkv_weight, "band", axis=1, tiled=True)
    w_out = lax.all_gather(out_weight, "band", axis=1, tiled=True)
    px = pixels.reshape(8, 8, 8, 7, 128).transpose(0, 1, 3, 2, 4).reshape(8, 8, 56, 128)
    square = spread(px, *prepare(embed, bpos, qkv, out, sscale, upw, downw, pool))
    rolled = lax.dynamic_slice(square, (0, shifts[1], 0), (8, 8, 768))
    row_index = lax.axis_index("row") * 8 + jnp.arange(8, dtype=jnp.int32)
    col_index = lax.axis_index("band") * 8 + jnp.arange(8, dtype=jnp.int32)
    row_region = (row_index >= lax.axis_size("row") * 8 - shifts[0]).astype(jnp.int32)
    col_region = (col_index >= lax.axis_size("band") * 8 - shifts[1]).astype(jnp.int32)
    labels = (2 * row_region[:, None] + col_region[None, :]).reshape(64)
    flat = rolled.reshape(64, 768)
    projected = jnp.dot(layer_normalize(flat), w_qkv, precision=highest_precision)
    mixed = window_attention(projected, labels[:, None] == labels[None, :], spat_scale)
    return (flat + jnp.dot(mixed, w_out, precision=highest_precision)).reshape(8, 8, 768)


def solution(mesh):
    P = jax.sharding.PartitionSpec
    return jax.shard_map(
        on_device,
        mesh=mesh,
        in_specs=(P("row", None, "band"), P(), P(), P(), P(), P(), P(), P(), P(),
                  P(None, "band"), P(None, "band"), P(), P()),
        out_specs=P("row", "band", None),
        check_vma=False,
    )
```

time: 245 us -> 202 us (0.82)
  Pallas kernels: 0 us -> 111 us
  matrix products: 100 us -> 18.7 us
  waiting for transfers between devices: 73.7 us -> 39 us
  starting transfers between devices: 30.1 us -> 0.08 us
  local copies, waits for them, and re-layouts: 15.8 us -> 3.46 us
  other arithmetic: 5.39 us -> 10.9 us
    pallas_call x0 -> x1, Pallas kernels: none -> 111 us  [spread(): pl.pallas_call(spread_kernel, out_shape=jax.ShapeDtypeStruct((8, 16, 768)...]
    dot_general x68 -> x4, matrix products: 100 us -> 18.7 us  [the longest x1 12.6 us: on_device(): jnp.dot(layer_normalize(flat), w_qkv, precision=highest_precision)]
    all_to_all x1 -> x0, waiting for transfers between devices: 63 us -> none  [on_device(): lax.all_to_all(pixels, 'band', split_axis=1, concat_axis=2, tiled=True)]
    all_gather x2, waiting for transfers between devices: 0.02 us -> 37.7 us  [the longest x1 31.6 us: on_device(): w_out = lax.all_gather(out_weight, 'band', axis=1, tiled=True)]
    ppermute x2 -> x0, starting transfers between devices: 19.7 us -> none  [from_behind(): return lax.ppermute(block, axis, route)]
    all_to_all x1 -> x0, starting transfers between devices: 10.5 us -> none  [on_device(): lax.all_to_all(pixels, 'band', split_axis=1, concat_axis=2, tiled=True)]
    ppermute x2 -> x0, waiting for transfers between devices: 9.26 us -> none  [from_behind(): return lax.ppermute(block, axis, route)]
    dynamic_slice x8 -> x0, local copies, waits for them, and re-layouts: 7.67 us -> none  [on_device(): lax.map(one_row, lax.all_to_all(pixels, 'band', split_axis=1, concat_axis...]
  transfers between devices with their start and end apart: 5 -> 2, of which waited for: 2 -> 2; matrix products, arithmetic and copies ran while one was open for 48% -> 14% of each run, Pallas kernels for 0% -> 55%
where the time goes in v1:
time: 202 us; the launch traced here: 200 us
  Pallas kernels  111 us (55%)
  waiting for transfers between devices  39 us (19%)
  matrix products  18.7 us (9%)
  between operations  17 us (8%)
  other arithmetic  10.9 us (5%)
  local copies, waits for them, and re-layouts  3.46 us (2%)
    pallas_call x1, Pallas kernels, spread(): pl.pallas_call(spread_kernel, out_shape=jax.ShapeDtypeStruct((8, 16, 768)...  111 us
    all_gather x1, waiting for transfers between devices, on_device(): w_out = lax.all_gather(out_weight, 'band', axis=1, tiled=True)  31.6 us
    dot_general x1, matrix products, on_device(): jnp.dot(layer_normalize(flat), w_qkv, precision=highest_precision)  12.6 us
    all_gather x1, waiting for transfers between devices, on_device(): w_qkv = lax.all_gather(qkv_weight, 'band', axis=1, tiled=True)  6.01 us
    unnamed x10, other arithmetic  4.72 us
    dot_general x1, matrix products, on_device(): jnp.dot(mixed, w_out, precision=highest_precision)  4.53 us
  transfers between devices with their start and end apart: 2, of which 2 were waited for; matrix products, arithmetic and copies ran while one was open for 14% of the time, Pallas kernels for 55%

profile of v1, /device:TPU:1, one launch (start us, length us, event | category | flops | bytes accessed | tf_op | source)
XLA Modules:
  0.0 200.1 jit_solution(10273493108295174639)
XLA Ops:
  6.5 0.0 all-gather.3.cloned.1.call-start
  6.6 0.7 all-gather.3.cloned.1.call-update
  7.3 0.0 all-gather.5.cloned.1.call-start
  7.3 0.7 all-gather.5.cloned.1.call-update
  8.1 0.7 broadcast_multiply_fusion.3
  8.7 0.1 broadcast_in_dim.10
  8.8 0.1 mul.76
  8.9 0.9 slice.27
  9.8 0.8 slice_multiply_fusion
  10.6 0.8 copy.21
  11.4 0.8 reduce_sum.55
  12.2 0.9 reduce_sum.54
  13.1 0.8 broadcast_subtract_fusion.2
  13.9 0.9 constant_dynamic-update-slice_fusion.4
  14.8 0.9 constant_dynamic-update-slice_fusion.3
  15.8 0.9 constant_dynamic-update-slice_fusion.2
  16.7 0.9 constant_dynamic-update-slice_fusion.1
  17.6 0.9 constant_dynamic-update-slice_fusion
  18.5 0.9 fusion.34.we
  19.5 0.1 copy.25
  19.6 0.1 copy.26
  19.7 0.1 broadcast_multiply_fusion
  19.8 0.2 mul.82
  20.1 0.1 copy.23
  20.2 0.1 reduce_sum.56
  20.3 0.1 broadcast_subtract_fusion
  20.4 0.1 reduce-precision_convert_fusion.2
  20.6 0.1 copy.22
  20.7 0.1 reshape.201
  20.7 0.1 reshape.200
  20.8 0.7 fusion.38
  24.1 0.1 broadcast_add_fusion
  24.1 0.1 add.93
  24.9 0.1 constant_dynamic-update-slice_fusion.9
  25.0 0.1 fusion.10
  25.2 0.1 fusion.3.wd
  25.3 0.0 copy-start.7
  25.4 111.0 %spread.1 = f32[8,16,768]{2,1,0:T(8,128)S(1)} custom-call(f32[8,8,56,128]{3,2,1,0:T(8,128)S(1)} %bitcast.45, bf16[768,256]{1,0:T(8,128)(2,1)S(1)} %fusion.34.we, f32[56,256]{1,0:T(8,128)S(1)} %pad_maximum_fusion.4.bp, bf16[384,256]{1,0:T(8,128)(2,1)S(1)} %fusion.35.wq, bf16[384,256]{1,0:T(8,128)(2,1)S(1)} %pad_maximum_fusion.1.wo, ...), custom_call_target="tpu_custom_call" | custom-call | tf_op jit(solution)/shard_map/spread/pallas_call | solution.py:244
  136.4 0.1 dynamic-slice_reduce_fusion
  136.5 0.2 multiply_reduce_fusion
  136.7 0.1 broadcast_compare_fusion
  136.8 6.0 %all-gather.3.cloned.1.call-done = f32[768,2304]{0,1:T(8,128)} async-done(((f32[768,288]{0,1:T(8,128)}), f32[768,2304]{0,1:T(8,128)}) %all-gather.3.cloned.1.call-update) | async-done | bytes 7077904 | tf_op jit(solution)/shard_map/all_gather | solution.py:279
  142.8 12.6 %fusion.11 = f32[64,3,12,64]{3,0,2,1:T(8,128)S(1)} fusion(f32[3,12,64,768]{3,2,1,0:T(8,128)} %bitcast.46, f32[8,16,768]{2,1,0:T(8,128)S(1)} %spread.1, s32[]{:T(128)S(6)} %select_n.7, f32[8,8]{1,0:T(8,128)S(1)} %add_rsqrt_fusion, f32[8,8]{1,0:T(8,128)S(1)} %broadcast_multiply_fusion.1), kind=kOutput, calls=%fused_computation.28 | convolution fusion | flops 1359052800 | bytes 7872516 | tf_op jit(solution)/shard_map/dot_general | solution.py:290
  155.4 0.8 fusion.39
  156.2 0.1 fusion.8
  156.3 0.8 fusion.6
  157.1 31.6 %all-gather.5.cloned.1.call-done = f32[768,768]{0,1:T(8,128)} async-done(((f32[768,96]{0,1:T(8,128)}), f32[768,768]{0,1:T(8,128)}) %all-gather.5.cloned.1.call-update) | async-done | bytes 2359312 | tf_op jit(solution)/shard_map/all_gather | solution.py:280
  188.8 4.5 %fusion.1 = f32[8,8,768]{2,1,0:T(8,128)} fusion(f32[64,768]{0,1:T(8,128)S(1)} %bitcast.47, f32[768,768]{0,1:T(8,128)} %all-gather.5.cloned.1.call-done, f32[8,16,768]{2,1,0:T(8,128)S(1)} %spread.1, s32[]{:T(128)S(6)} %select_n.7), kind=kOutput, calls=%fused_computation.3 | convolution fusion | flops 453033984 | bytes 2949124 | tf_op jit(solution)/shard_map/dot_general | solution.py:292
  (36 shorter events, 0.3 us)
Async XLA Ops:
  6.5 14.0 %copy-start.2 = (f32[112,64]{0,1:T(8,128)S(1)}, f32[112,64]{0,1:T(8,128)}, u32[]{:S(2)}) copy-start(f32[112,64]{0,1:T(8,128)} %param.15) | copy-start | bytes 86020
  6.5 12.9 %copy-start.5 = (f32[12,112]{1,0:T(8,128)S(1)}, f32[12,112]{1,0:T(8,128)}, u32[]{:S(2)}) copy-start(f32[12,112]{1,0:T(8,128)} %param.21) | copy-start | bytes 16132
  6.5 13.5 %copy-start.3 = (f32[256,64]{0,1:T(8,128)S(1)}, f32[256,64]{0,1:T(8,128)}, u32[]{:S(2)}) copy-start(f32[256,64]{0,1:T(8,128)} %param.20) | copy-start | bytes 196612
  6.5 13.6 %copy-start.1 = (f32[64,64]{1,0:T(8,128)S(1)}, f32[64,64]{1,0:T(8,128)}, u32[]{:S(2)}) copy-start(f32[64,64]{1,0:T(8,128)} %param.17) | copy-start | bytes 49156
  6.5 14.0 %copy-start.4 = (f32[64,256]{1,0:T(8,128)S(1)}, f32[64,256]{1,0:T(8,128)}, u32[]{:S(2)}) copy-start(f32[64,256]{1,0:T(8,128)} %param.19) | copy-start | bytes 196612
  6.5 136.3 %all-gather.3.cloned.1.call-start = ((), (), s32[]{:S(2)}) async-start(), calls=%async_computation | async-start | bytes 7962624 | tf_op jit(solution)/shard_map/all_gather | solution.py:279
  7.3 13.5 %copy-start.6 = (s32[2]{0:T(128)S(1)}, s32[2]{0:T(128)}, u32[]{:S(2)}) copy-start(s32[2]{0:T(128)} %param.25) | copy-start | bytes 28
  7.3 181.5 %all-gather.5.cloned.1.call-start = ((), (), s32[]{:S(2)}) async-start(), calls=%async_computation.1 | async-start | bytes 2654208 | tf_op jit(solution)/shard_map/all_gather | solution.py:280
  20.4 5.0 %copy-start = (f32[8,64,896]{2,1,0:T(8,128)S(1)}, f32[8,64,896]{2,1,0:T(8,128)}, u32[]{:S(2)}) copy-start(f32[8,64,896]{2,1,0:T(8,128)} %param.13) | copy-start | bytes 5505028
  25.3 111.4 %copy-start.7 = (f32[12]{0:T(128)S(1)}, f32[12]{0:T(128)}, u32[]{:S(2)}) copy-start(f32[12]{0:T(128)} %param.24) | copy-start | bytes 148
Sparse Core Ops, SparseCore 0:
  9.4 133.3 all-gather.2
  144.9 43.8 all-gather.4

commit v2 on v1

v2 whole, which is shorter than its diff:
```python
import math
import jax, jax.numpy as jnp
from jax import lax
from jax.experimental import pallas as pl
from jax.experimental.pallas import tpu as pltpu

F32, BF16 = jnp.float32, jnp.bfloat16
EPS = 1e-05

def parts(x, n):
    out = []
    for i in range(n):
        p = x.astype(BF16)
        out.append(p)
        if i < n - 1:
            x = x - p.astype(F32)
    return out

def lhs6(x, axis=1):
    a, b, c = parts(x, 3)
    return jnp.concatenate([a, b, c, a, b, a], axis)

def lhs3(x, axis=1):
    a, b = parts(x, 2)
    return jnp.concatenate([a, b, a], axis)

def mm(a, b, ca=1, cb=0):
    return lax.dot_general(a, b, (((ca,), (cb,)), ((), ())), preferred_element_type=F32)

def bd(w):
    z = jnp.zeros_like(w)
    return jnp.concatenate([jnp.concatenate([w, z], 1), jnp.concatenate([z, w], 1)], 0)

def prepare(embed, bpos_t, qkv, wout, sscale, upw, down_t, pool, bs, we, bp, wq, wo, wu, wd, gp):
    cat = jnp.concatenate
    cent = lambda w: w - jnp.mean(w, axis=1, keepdims=True)

    def put(ref, cols, w, order):
        n = w.shape[0]
        ps = parts(w, max(order) + 1)
        for i, j in enumerate(order):
            ref[n * i:n * i + n, cols] = ps[j]
    e = embed[...]
    put(we, slice(0, 128), bd(e), (0, 0, 0, 1, 1, 2))
    put(we, slice(128, 256), bd(cent(e)), (0, 0, 0, 1, 1, 2))
    b = bpos_t[...].T
    bs[...] = cat([b, cent(b)], 1)
    even, odd = bs[pl.ds(0, 56, stride=2), :], bs[pl.ds(1, 56, stride=2), :]
    bp[...] = cat([even[:, :64], odd[:, :64], even[:, 64:], odd[:, 64:]], 1)
    w = qkv[...]
    lane = lax.broadcasted_iota(jnp.int32, (64, 64), 1) // 16
    qs = jnp.where(lane < 2, jnp.where(lane == 0, sscale[0], sscale[1]), jnp.where(lane == 2, sscale[2], sscale[3]))
    q = w[:, :64] * (qs * (math.log2(math.e) / 4.0))
    put(wq, slice(0, 256), cat([q, w[:, 64:128], w[:, 128:], w[:, 128:]], 1), (0, 0, 1, 1, 0, 2))
    o = wout[...]
    put(wo, slice(0, 128), bd(o), (0, 0, 1))
    put(wo, slice(128, 256), bd(cent(o)), (0, 0, 1))
    put(wu, slice(0, 256), upw[...], (0, 0, 1, 1))
    d = bd(down_t[...].T)
    d1, d2 = parts(d, 2)
    wd[0:512, 0:128] = d1
    wd[512:1024, 0:128] = d1
    wd[0:512, 128:256] = d2
    wd[512:1024, 128:256] = jnp.zeros((512, 128), BF16)
    p1, p2 = parts(pool[...], 2)
    bi = lax.broadcasted_iota(jnp.int32, (112, 448), 0)
    ti = lax.broadcasted_iota(jnp.int32, (112, 448), 1)
    own = lax.broadcasted_iota(jnp.int32, (8, 448), 1) // 56 == lax.broadcasted_iota(jnp.int32, (8, 448), 0)
    for b2 in range(2):
        sel = jnp.where(bi == 2 * (ti % 56) + b2, 1.0, 0.0).astype(BF16)
        for i, p in enumerate((p1, p2)):
            g = mm(p, sel)
            for j in range(0, 12, 2):
                for t in (j, j + 1):
                    rows = jnp.where(own, jnp.broadcast_to(g[t:t + 1], (8, 448)), 0.0)
                    gp[i, pl.ds((t * 2 + b2) * 8, 8), :] = rows.astype(BF16)


def gelu(v):
    return 0.5 * v * (1.0 + jnp.tanh(math.sqrt(2 / math.pi) * (v + 0.044715 * (v * v * v))))

def row_tokens(load, we_ref, bp_ref, wq_ref, wo_ref, wu_ref, wd_ref, gp_ref):
    NP = 8
    cat = jnp.concatenate
    x = cat([load(p) for p in range(NP)], 0)
    bpt = cat([bp_ref[...]] * NP, 0)
    t = mm(lhs6(x), we_ref[...]) + bpt
    tok, tokc = t[:, :128], t[:, 128:]
    r_i = lax.broadcasted_iota(jnp.int32, (128, 128), 0) // 64
    c_i = lax.broadcasted_iota(jnp.int32, (128, 128), 1) // 64
    avg = jnp.where(r_i == c_i, 1.0 / 64, 0.0).astype(BF16)
    avg = cat([avg, avg], 0)
    low = lax.broadcasted_iota(jnp.int32, (448, 128), 1) < 64

    def norm(c):
        var = mm(cat(parts(c * c, 2), 1), avg)
        return c * lax.rsqrt(var + EPS)

    def split_bands(n, k):
        ps = [a.astype(F32) for a in parts(n, k)]
        rs = [pltpu.roll(a, 64, 1) for a in ps]
        pairs = [(0, 1)] + ([(2, 0)] if k == 3 else [])
        b0 = [jnp.where(low, ps[i], rs[j]).astype(BF16) for i, j in pairs]
        b1 = [jnp.where(low, rs[i], ps[j]).astype(BF16) for i, j in pairs]
        return cat([cat([b[0]] + b, 1) for b in (b0, b1)], 0)

    qkv = mm(split_bands(norm(tokc), 3), wq_ref[...])
    lane = lax.broadcasted_iota(jnp.int32, (1, 128), 1)
    lowp = lax.broadcasted_iota(jnp.int32, (112, 128), 1) < 64
    mlow = jnp.where(lane < 64, 1.0, 0.0).astype(BF16)
    mhigh = jnp.where(lane < 64, 0.0, 1.0).astype(BF16)
    hm = [jnp.where((lane // 16) % 4 == h, 1.0, 0.0).astype(BF16) for h in range(4)]
    row128 = lax.broadcasted_iota(jnp.int32, (128, 112), 0)
    mixes = []
    for p in range(NP):
        def both(sl):
            return cat([qkv[56 * p:56 * p + 56, sl], qkv[448 + 56 * p:504 + 56 * p, sl]], 0)
        qk, v = both(slice(0, 128)), both(slice(128, 256))
        kq = pltpu.roll(qk, 64, 1)
        q1, q2, q3 = parts(jnp.where(lowp, qk, kq), 3)
        k1, k2, k3 = parts(jnp.where(lowp, kq, qk), 3)
        kl = k1 * mlow + k2 * mhigh
        lhs = cat([kl, kl, k1 * mlow + k3 * mhigh], 1)
        qc = cat([q1, q2, q3 * mlow + q1 * mhigh], 1)
        pad = jnp.zeros((16, 384), BF16)
        heads = []
        for h in range(4):
            heads += [qc * cat([hm[h]] * 3, 1), pad]
        st = mm(lhs, cat(heads, 0), 1, 1)
        m = jnp.max(st, axis=0, keepdims=True)
        e = jnp.exp2(st - m)
        s = jnp.sum(e, axis=0, keepdims=True)
        e1, e2 = parts(e, 2)
        vt = v.T
        vh = vt.astype(BF16).astype(F32)
        vs = jnp.where(row128 < 64, vh, vt - vh).astype(BF16)
        r = mm(vs, e1)
        r2 = mm(vs[:64], e2)
        inv = 1.0 / s
        ot = []
        for h in range(4):
            sl = slice(128 * h, 128 * h + 128)
            o = r[16 * h:16 * h + 16, sl] + r[64 + 16 * h:80 + 16 * h, sl] + r2[16 * h:16 * h + 16, sl]
            ot.append(o * inv[:, sl])
        mt = cat(ot, 0)
        mt = cat([mt, pltpu.roll(mt, 72, 1)], 0)
        mixes.append(mt.T[:56])
    mix = cat(mixes, 0)
    o = mm(lhs3(mix), wo_ref[...])
    n2 = norm(tokc + o[:, 128:])
    h = gelu(mm(split_bands(n2, 2), wu_ref[...]))
    h1, h2 = parts(h, 2)
    hc = cat([h1[:448], h1[448:], h2[:448], h2[448:]], 1)
    d = mm(hc, wd_ref[...])
    y = tok + o[:, :128] + (d[:, :128] + d[:, 128:])
    y1, y2 = parts(y, 2)
    r = mm(gp_ref[0], cat([y1, y2], 1))
    r = (r[:, :128] + r[:, 128:]) + mm(gp_ref[1], y1)
    lo8 = lax.broadcasted_iota(jnp.int32, (8, 128), 1) < 64
    outs = []
    for j in range(6):
        g = lambda a, b: r[((2 * j + a) * 2 + b) * 8:((2 * j + a) * 2 + b) * 8 + 8]
        outs.append(jnp.where(lo8, g(0, 0) + pltpu.roll(g(0, 1), 64, 1),
                              pltpu.roll(g(1, 0), 64, 1) + g(1, 1)))
    return cat(outs, 1)


def window(square, shifts, scale, wg, out):
    cat = jnp.concatenate
    nb, nr = lax.axis_size("band"), lax.axis_size("row")
    shift = shifts[1]
    zr = square[:, 7:15, :]
    for i in range(1, 7):
        zr = jnp.where(shift == i, square[:, i:i + 8, :], zr)
    zr = zr.reshape(64, 768)
    c = zr - jnp.mean(zr, axis=1, keepdims=True)
    n = c * lax.rsqrt(jnp.mean(c * c, axis=1, keepdims=True) + EPS)
    n1, n2, n3 = parts(n, 3)
    n123, n12 = cat([n1, n2, n3], 0), cat([n1, n2], 0)

    def proj(t, full):
        w = parts(cat([wg[j % 12, j // 12] for j in range(16 * t, 16 * t + 16)], 0), 3 if full else 2)
        if full:
            a, b = mm(n123, w[0], 1, 1), mm(n12, w[1], 1, 1)
            return (a[:64] + (a[64:128] + b[:64])) + (a[128:] + b[64:] + mm(n1, w[2], 1, 1))
        a = mm(n12, w[0], 1, 1)
        return a[:64] + (a[64:] + mm(n1, w[1], 1, 1))

    t_i = lax.broadcasted_iota(jnp.int32, (64, 128), 0)
    q_i = lax.broadcasted_iota(jnp.int32, (64, 128), 1) % 64
    low = lax.broadcasted_iota(jnp.int32, (64, 128), 1) < 64
    row0 = lax.axis_index("row") * 8
    col0 = lax.axis_index("band") * 8

    def region(t):
        r = jnp.where(row0 + t // 8 >= nr * 8 - shifts[0], 2, 0)
        return r + jnp.where(col0 + t % 8 >= nb * 8 - shift, 1, 0)
    same = region(t_i) == region(q_i)
    mixed = []
    for half in range(2):
        q, k, v = proj(half, True), proj(2 + half, True), proj(4 + half, False)
        for i in range(3):
            pair = 3 * half + i
            sl = slice(128 * i, 128 * i + 128)
            qp, kp, vp = q[:, sl], k[:, sl], v[:, sl]
            a1, a2, a3 = parts(cat([jnp.where(low, qp, 0.0), jnp.where(low, 0.0, qp)], 0), 3)
            k1, k2, k3 = parts(kp, 3)
            st = mm(cat([k1, k1, k1, k2, k2, k3], 1), cat([a1, a2, a3, a1, a2, a1], 1), 1, 1)
            f = math.log2(math.e) / 8.0
            st = st * jnp.where(low, scale[2 * pair] * f, scale[2 * pair + 1] * f)
            st = jnp.where(same, st, -1e30)
            e = jnp.exp2(st - jnp.max(st, axis=0, keepdims=True))
            a = e * (1.0 / jnp.sum(e, axis=0, keepdims=True))
            p1, p2 = parts(a.T, 2)
            v1, v2 = parts(vp, 2)
            r = mm(cat([p1, p2], 0), v1)
            r = r[:128] + (r[128:] + mm(p1, v2))
            mixed.append(jnp.where(low, r[:64], r[64:]))
    o1, o2 = parts(cat(mixed, 1), 2)
    o12 = cat([o1, o2], 0)
    for t in range(2):
        w = parts(cat([wg[12 + j % 4, j // 4] for j in range(16 * t, 16 * t + 16)], 0), 2)
        a = mm(o12, w[0], 1, 1)
        res = zr[:, 384 * t:384 * t + 384] + (a[:64] + (a[64:] + mm(o1, w[1], 1, 1)))
        out[:, :, 384 * t:384 * t + 384] = res.reshape(8, 8, 384)


ORDER = (4, 3, 5, 2, 6, 1, 7)
MESH = pl.DeviceIdType.MESH


def block_kernel(px, wcat, embed, bpos_t, qkv, wout, sscale, upw, down_t, pool, scale, shifts, out,
                 bs, we, bp, wq, wo, wu, wd, gp, xbuf, zs, square, wg,
                 lsem, ssem, rsem, zsem, zrem, fsem, frem, osem, ysem, yrem, gsem, grem):
    nb, nr = lax.axis_size("band"), lax.axis_size("row")
    me, row = lax.axis_index("band"), lax.axis_index("row")
    up, down = lax.rem(row + nr - 1, nr), lax.rem(row + 1, nr)
    left = lax.rem(me + nb - 1, nb)
    yl, core = me // 2, lax.rem(me, 2)
    yh, x, zc = lax.rem(row, 2), lax.rem(row // 2, 4), row // 8
    zb = lax.rem(zc, 2)
    y = yh * 4 + yl

    def chip_y(d, c):
        t = lax.rem(y + d + 8, 8)
        return {"band": lax.rem(t, 4) * 2 + c, "row": row - yh + t // 4}

    def chip_x(d):
        return {"band": me, "row": zc * 8 + lax.rem(x + d + 4, 4) * 2 + yh}
    chip_z = {"band": me, "row": row + 8 * (1 - 2 * zb)}
    other = {"band": me + 1 - 2 * core, "row": row}

    def piece(x_, zb_, c_):
        return (lax.rem(x_ + 4, 4) * 2 + zb_) * 2 + c_

    barrier = pltpu.get_barrier_semaphore()

    def greet(to):
        pl.semaphore_signal(barrier, inc=1, device_id=to, device_id_type=MESH)
    for k in range(1, nb):
        greet({"band": lax.rem(me + k, nb), "row": row})
    greet({"band": me, "row": down})
    for c in range(2):
        greet(chip_y(-1, c))
        greet(chip_y(1, c))
    greet(chip_y(-2, 0))
    greet(chip_y(2, 1))
    greet(chip_z)
    greet(chip_x(-1))
    greet(chip_x(1))

    def remote(src, dst, send, recv, to):
        return pltpu.make_async_remote_copy(src_ref=src, dst_ref=dst, send_sem=send, recv_sem=recv,
                                            device_id=to, device_id_type=MESH)

    def own(r):
        return pltpu.make_async_copy(px.at[r, me], xbuf.at[r, pl.ds(me * 56, 56)], lsem.at[r])

    def hop(r, k):
        to = lax.rem(me + k, nb)
        return remote(px.at[r, to], xbuf.at[r, pl.ds(me * 56, 56)], ssem.at[r, k], rsem.at[r, k],
                      {"band": to, "row": row})

    def rise(r):
        return remote(zs.at[r], square.at[r + 1, pl.ds(0, 8)], zsem.at[r], zrem.at[r], {"band": me, "row": up})

    def side(r):
        return remote(square.at[r, pl.ds(0, 8)], square.at[r, pl.ds(8, 8)], fsem.at[r], frem.at[r],
                      {"band": left, "row": row})

    def deal(i, c):
        to = chip_y((1, -1, 2 - 4 * core)[i], c)
        s = piece(x, zb, c)
        return remote(wcat.at[pl.ds(s * 24, 24)], wg.at[s, me], ysem.at[i, c], yrem.at[i, core], to)

    def dealt(i, c):
        b = lax.rem(yl + (3, 1, 2)[i], 4) * 2 + c
        return remote(wcat.at[pl.ds(0, 24)], wg.at[piece(x, zb, core), b], ysem.at[i, c], yrem.at[i, c], other)

    def deal_other(s):
        return remote(wcat.at[pl.ds(s * 24, 24)], wg.at[s, me], ysem.at[3, 0], yrem.at[3, 0], other)
    mine = piece(x, zb, core)
    keep = pltpu.make_async_copy(wcat.at[pl.ds(mine * 24, 24)], wg.at[mine, me], osem)

    def pass_on(s, lo, n, i, to):
        ref = wg.at[s, pl.ds(lo, n)]
        return remote(ref, ref, gsem.at[i], grem.at[i], to)
    zo = 1 - zb
    GOT = {"Z": (0, 0, zo, 0, 8), "M0": (1, -1, zb, 0, 8), "P0": (2, 1, zb, 0, 8), "M1": (3, -1, zo, 0, 8),
           "P1": (4, 1, zo, 0, 8), "RM0": (5, 2, zb, 0, 4), "RP0": (6, 2, zb, 4, 4), "RM1": (7, 2, zo, 0, 4),
           "RP1": (8, 2, zo, 4, 4), "O": (9, 0, zb, 0, 8)}

    def got(name):
        i, dx, z, lo, n = GOT[name]
        return pass_on(piece(x + dx, z, core), lo, n, i, other)

    def to_other(name):
        i, dx, z, lo, n = GOT[name]
        return pass_on(piece(x + dx, z, core), lo, n, 10 + i, other)

    def from_other(name):
        i, dx, z, lo, n = GOT[name]
        return pass_on(piece(x + dx, z, 1 - core), lo, n, 10 + i, other)
    def send(name):
        if name == "Z":
            return pass_on(mine, 0, 8, 0, chip_z)
        if name in ("M0", "M1"):
            return pass_on(piece(x, zb if name == "M0" else zo, core), 0, 8, 1 if name == "M0" else 3, chip_x(1))
        if name in ("P0", "P1"):
            return pass_on(piece(x, zb if name == "P0" else zo, core), 0, 8, 2 if name == "P0" else 4, chip_x(-1))
        z = zb if name[2] == "0" else zo
        if name[1] == "M":
            return pass_on(piece(x - 1, z, core), 0, 4, 5 if name == "RM0" else 7, chip_x(1))
        return pass_on(piece(x + 1, z, core), 4, 4, 6 if name == "RP0" else 8, chip_x(-1))

    def start_own(r, c):
        own(r).start()
        return c
    lax.fori_loop(0, 8, start_own, 0)
    keep.start()
    pl.semaphore_wait(barrier, nb + 9)

    def start_row(r, c):
        for k in ORDER:
            hop(r, k).start()
        return c
    start_row(0, 0)
    for i in range(3):
        for c in range(2):
            deal(i, c).start()
    deal_other(piece(x, zb, 1 - core)).start()
    lax.fori_loop(1, 8, start_row, 0)
    prepare(embed, bpos_t, qkv, wout, sscale, upw, down_t, pool, bs, we, bp, wq, wo, wu, wd, gp)

    def weights(step):
        if step == 0:
            keep.wait()
            for i in range(3):
                for c in range(2):
                    dealt(i, c).wait_recv()
            remote(wcat.at[pl.ds(0, 24)], wg.at[mine, me + 1 - 2 * core], ysem.at[3, 0], yrem.at[3, 0], other).wait_recv()
            for name in ("Z", "M0", "P0"):
                send(name).start()
            to_other("O").start()
        if step == 2:
            got("Z").wait_recv()
            send("M1").start()
            send("P1").start()
            to_other("Z").start()
        if step == 3:
            for name, relay in (("M0", "RM0"), ("P0", "RP0")):
                got(name).wait_recv()
                send(relay).start()
                to_other(name).start()
        if step == 5:
            for name, relay in (("M1", "RM1"), ("P1", "RP1")):
                got(name).wait_recv()
                send(relay).start()
                to_other(name).start()
        if step == 6:
            for name in ("RM0", "RP0"):
                got(name).wait_recv()
                to_other(name).start()
        if step == 8:
            for name in ("RM1", "RP1"):
                got(name).wait_recv()
                to_other(name).start()

    def one(r, c):
        own(r).wait()
        for k in range(1, nb):
            hop(r, k).wait_recv()
        z = row_tokens(lambda p: xbuf[r, pl.ds(p, 56, stride=8), :], we, bp, wq, wo, wu, wd, gp)

        @pl.when(r < 7)
        def _():
            zs[r] = z
            rise(r).start()

        @pl.when(r == 7)
        def _():
            square[0, 0:8] = z
            side(0).start()

        @pl.when(r > 0)
        def _():
            rise(r - 1).wait_recv()
            side(r).start()
        for step in (0, 2, 3, 5, 6):
            @pl.when(r == step)
            def _():
                weights(step)
        return c
    lax.fori_loop(0, 8, one, 0)
    weights(8)

    def arrived(r, c):
        side(r).wait_recv()
        return c
    lax.fori_loop(0, 8, arrived, 0)
    for name in GOT:
        from_other(name).wait_recv()
    window(square, shifts, scale, wg, out)

    def finish(r, c):
        for k in range(1, nb):
            hop(r, k).wait_send()
        side(r).wait_send()

        @pl.when(r < 7)
        def _():
            rise(r).wait_send()
        return c
    lax.fori_loop(0, 8, finish, 0)
    for i in range(3):
        for c in range(2):
            deal(i, c).wait_send()
    deal_other(piece(x, zb, 1 - core)).wait_send()
    for name in GOT:
        to_other(name).wait_send()
        if name != "O":
            send(name).wait_send()


def block(*args):
    V, S, A = (pl.BlockSpec(memory_space=m) for m in (pltpu.VMEM, pltpu.SMEM, pl.ANY))
    D = pltpu.SemaphoreType.DMA
    B = lambda *s: pltpu.VMEM(s, BF16)
    M = lambda *s: pltpu.VMEM(s, F32)
    return pl.pallas_call(
        block_kernel,
        out_shape=jax.ShapeDtypeStruct((8, 8, 768), F32),
        in_specs=[A, A, V, V, V, V, S, V, V, V, S, S],
        out_specs=V,
        scratch_shapes=[M(112, 128), B(768, 256), M(56, 256), B(384, 256), B(384, 256), B(256, 256),
                        B(1024, 256), B(2, 192, 448),
                        M(8, 448, 128), M(8, 8, 768), M(8, 16, 768), M(16, 8, 24, 768),
                        D((8,)), D((8, 8)), D((8, 8)), D((8,)), D((8,)), D((8,)), D((8,)), D,
                        D((4, 2)), D((4, 2)), D((20,)), D((20,))],
        compiler_params=pltpu.CompilerParams(collective_id=0, has_side_effects=True,
                                             vmem_limit_bytes=56 * 2 ** 20),
        name="block",
    )(*args)


def on_device(pixels, embed, bpos, qkv, wout, sscale, upw, down, pool, qkv_weight, out_weight, spat_scale, shifts):
    px = pixels.reshape(8, 8, 8, 7, 128).transpose(0, 1, 3, 2, 4).reshape(8, 8, 56, 128)
    wcat = jnp.concatenate([qkv_weight.T, out_weight.T], 0)
    return block(px, wcat, embed, bpos.T, qkv, wout, sscale, upw, down.T, pool, spat_scale, shifts)


def solution(mesh):
    P = jax.sharding.PartitionSpec
    return jax.shard_map(
        on_device,
        mesh=mesh,
        in_specs=(P("row", None, "band"), P(), P(), P(), P(), P(), P(), P(), P(),
                  P(None, "band"), P(None, "band"), P(), P()),
        out_specs=P("row", "band", None),
        check_vma=False,
    )
```

time: 202 us -> 110 us (0.54)
  the two profiles are of different devices: /device:TPU:1 before, /device:TPU:9 now
where the time goes in v2:
time: 110 us
  Pallas kernels  106 us (96%)
  other arithmetic  2.35 us (2%)
  local copies, waits for them, and re-layouts  1.62 us (1%)
    pallas_call x1, Pallas kernels, block(): pl.pallas_call(block_kernel, out_shape=jax.ShapeDtypeStruct((8, 8, 768),...  106 us
    concatenate x1, other arithmetic, on_device(): wcat = jnp.concatenate([qkv_weight.T, out_weight.T], 0)  2.35 us

profile of v2, /device:TPU:9, one launch (start us, length us, event | category | flops | bytes accessed | tf_op | source)
XLA Modules:
  0.0 109.9 jit_solution(380929289375696378)
XLA Ops:
  0.0 2.3 %pad_maximum_fusion.wcat = f32[384,768]{1,0:T(8,128)} fusion(f32[96,768]{1,0:T(8,128)} %bitcast.11, f32[288,768]{1,0:T(8,128)} %bitcast.10), kind=kLoop, calls=%fused_computation | loop fusion | flops 294912 | bytes 2359296 | tf_op jit(solution)/shard_map/concatenate | solution.py:468
  2.3 106.0 %block.1 = f32[8,8,768]{2,1,0:T(8,128)} custom-call(f32[8,8,56,128]{3,2,1,0:T(8,128)} %bitcast.9, f32[384,768]{1,0:T(8,128)} %pad_maximum_fusion.wcat, f32[64,64]{1,0:T(8,128)} %embed.1, f32[64,112]{1,0:T(8,128)} %bitcast.13, f32[64,192]{1,0:T(8,128)} %qkv.1, f32[64,64]{1,0:T(8,128)} %wout.1, f32[4]{0:T(128)} %sscale.1, f32[64,256]{1,0:T(8,128)} %upw.1, ...), custom_call_target="tpu_custom_call" | custom-call | tf_op jit(solution)/shard_map/block/pallas_call | solution.py:450
  108.3 1.6 %copy.15 = f32[8,8,768]{2,1,0:T(8,128)} copy(f32[8,8,768]{2,1,0:T(8,128)} %block.1) | data formatting | bytes 393216
